TPU v7x, 128 devices: a whole 4x4x4 slice. The times are simulated.
128 devices in a mesh: ctx: 32 (over y, x, z_lo), batch: 4 (over z_hi, core).
Axes of the slice: x: 4, y: 4, z: 4 (z_hi: 2, z_lo: 2; z = z_hi * 2 + z_lo), core: 2. Of those that a mesh axis runs over, the one named last changes fastest.
Arguments:
- queries: bfloat16 [4, 8192, 2048], P('batch', 'ctx'), may hold values from -120 to 120
- keys: bfloat16 [4, 8192, 512], P('batch', 'ctx'), may hold values from -6 to 6
- values: bfloat16 [4, 8192, 512], P('batch', 'ctx'), may hold values from -6 to 6
- tau: float32 [16], replicated, may hold values from 0.5 to 2
- out_grad: bfloat16 [4, 8192, 2048], P('batch', 'ctx'), may hold values from -18 to 18
- key_blocks: int32 [4, 64, 13], replicated, may hold values from 0 to 63, as said below
Outputs:
- attended: bfloat16 [4, 8192, 2048], P('batch', 'ctx')
- query_grad: bfloat16 [4, 8192, 2048], P('batch', 'ctx')
- key_grad: bfloat16 [4, 8192, 512], P('batch', 'ctx')
- value_grad: bfloat16 [4, 8192, 512], P('batch', 'ctx')
- tau_grad: float32 [16], replicated
Inputs may be any that keep to these rules, and one draw needn't show every extreme that they name: `key_blocks`: row a of head group g lists a - 1, a, a + 1, then a + m s and a - m s for m = 1 to 5, all modulo 64, with a stride s of 2 or 3 drawn for each group and row.
All inputs are finite; a program needn't handle non-finite values.
Results may differ from a plain program's by a relative error of at most 0.0051.
Values may be sent and summed in bfloat16 or wider, within the bound.
A program may use at most 192 MiB of HBM per device.

v0:
```python
import math
import jax
import jax.numpy as jnp
from jax import lax
from jax.sharding import PartitionSpec as P

HEADS = 16
KV_HEADS = 4
HD = 128
BLOCK = 128


def passed_along(block, axis, distance):
    devices = range(lax.axis_size(axis))
    route = [((i - distance) % len(devices), i) for i in devices]
    return lax.ppermute(block, axis, route)


def body(queries, keys, values, tau, out_grad, key_blocks):
    ctx_size = lax.axis_size("ctx")
    myself = lax.axis_index("ctx")
    tokens = queries.shape[1]
    local_blocks = tokens // BLOCK
    listed_count = key_blocks.shape[2]
    block_reach = 3 * ((listed_count - 3) // 2)
    reach_dev = min((local_blocks - 1 + block_reach) // local_blocks, ctx_size // 2)
    slot_count = 2 * reach_dev + 1
    per_group = HEADS // KV_HEADS
    root_hd = math.sqrt(HD)
    paired = jnp.stack([keys[0], values[0]])
    window = jnp.zeros((2, slot_count, tokens, KV_HEADS * HD), jnp.bfloat16)
    farthest = passed_along(paired, "ctx", -reach_dev)
    window = lax.dynamic_update_slice_in_dim(window, farthest[:, None], slot_count - 1, 1)

    def walk_turn(turn_no, state_in):
        current, filled = state_in
        current = passed_along(current, "ctx", 1)
        filled = lax.dynamic_update_slice_in_dim(
            filled, current[:, None], slot_count - 1 - turn_no, 1
        )
        return (current, filled)

    window = lax.fori_loop(1, slot_count, walk_turn, (farthest, window))[1]
    blocks_all = window.reshape(2, slot_count * local_blocks, BLOCK, KV_HEADS, HD)
    own_lists = lax.dynamic_slice_in_dim(key_blocks, myself * local_blocks, local_blocks, 1)
    window_index = (
        own_lists // local_blocks - myself + reach_dev
    ) % ctx_size * local_blocks + own_lists % local_blocks
    window_ids = jnp.arange(slot_count * local_blocks, dtype=jnp.int32)
    query_all = queries[0].reshape(local_blocks, BLOCK, KV_HEADS, per_group, HD)
    grad_all = out_grad[0].reshape(local_blocks, BLOCK, KV_HEADS, per_group, HD)
    factor = tau.reshape(KV_HEADS, per_group) / root_hd
    results = []
    query_parts = []
    placed_parts = []
    scale_parts = []
    for group_id in range(KV_HEADS):
        picks = window_index[group_id].reshape(-1)
        key_rows = jnp.take(blocks_all[0, :, :, group_id], picks, axis=0).reshape(
            local_blocks, listed_count * BLOCK, HD
        )
        value_rows = jnp.take(blocks_all[1, :, :, group_id], picks, axis=0).reshape(
            local_blocks, listed_count * BLOCK, HD
        )
        query_rows = query_all[:, :, group_id]
        grad_rows = grad_all[:, :, group_id]
        scale_row = factor[group_id]
        raw_scores = jnp.einsum(
            "nqhd,nkd->nhqk", query_rows, key_rows, preferred_element_type=jnp.float32
        )
        weights = jax.nn.softmax(raw_scores * scale_row[None, :, None, None], axis=-1)
        probs_low = weights.astype(jnp.bfloat16)
        result = jnp.einsum(
            "nhqk,nkd->nqhd", probs_low, value_rows, preferred_element_type=jnp.float32
        )
        row_dot = jnp.sum(grad_rows.astype(jnp.float32) * result, axis=-1)
        dweights = jnp.einsum(
            "nqhd,nkd->nhqk", grad_rows, value_rows, preferred_element_type=jnp.float32
        )
        dscores = weights * (dweights - row_dot.transpose(0, 2, 1)[..., None])
        scale_parts.append(jnp.sum(dscores * raw_scores, axis=(0, 2, 3)) / root_hd)
        scaled = (dscores * scale_row[None, :, None, None]).astype(jnp.bfloat16)
        query_part = jnp.einsum(
            "nhqk,nkd->nqhd", scaled, key_rows, preferred_element_type=jnp.float32
        )
        key_part = jnp.einsum(
            "nhqk,nqhd->nkd", scaled, query_rows, preferred_element_type=jnp.float32
        )
        value_part = jnp.einsum(
            "nhqk,nqhd->nkd", probs_low, grad_rows, preferred_element_type=jnp.float32
        )
        chooser = (picks[:, None] == window_ids[None, :]).astype(jnp.float32)
        both_parts = jnp.stack([key_part, value_part]).reshape(
            2, local_blocks * listed_count, BLOCK * HD
        )
        placed_parts.append(
            jnp.einsum("sw,csx->cwx", chooser, both_parts, precision=lax.Precision.HIGHEST)
        )
        results.append(result)
        query_parts.append(query_part)
    attended = jnp.stack(results, axis=2).reshape(1, tokens, HEADS * HD).astype(jnp.bfloat16)
    query_grad = jnp.stack(query_parts, axis=2).reshape(1, tokens, HEADS * HD).astype(jnp.bfloat16)
    stacked = jnp.stack(placed_parts).reshape(KV_HEADS, 2, slot_count, local_blocks, BLOCK, HD)
    grads_window = stacked.transpose(2, 1, 3, 4, 0, 5).reshape(slot_count, 2, tokens, KV_HEADS * HD)

    def chain_turn(turn_no, partial_sum):
        moved = passed_along(partial_sum, "ctx", -1)
        return moved + lax.dynamic_index_in_dim(grads_window, turn_no, 0, keepdims=False)

    partial_sum = lax.fori_loop(1, slot_count, chain_turn, grads_window[0])
    summed = passed_along(partial_sum.astype(jnp.bfloat16), "ctx", reach_dev).astype(
        partial_sum.dtype
    )
    key_grad = summed[0].reshape(1, tokens, KV_HEADS * HD).astype(jnp.bfloat16)
    value_grad = summed[1].reshape(1, tokens, KV_HEADS * HD).astype(jnp.bfloat16)
    scale_total = lax.psum(jnp.stack(scale_parts), ("ctx", "batch"))
    tau_grad = scale_total.reshape(HEADS) / math.sqrt(lax.axis_size("batch") * ctx_size * tokens)
    return (attended, query_grad, key_grad, value_grad, tau_grad)


def solution(mesh):
    return jax.shard_map(
        body,
        mesh=mesh,
        in_specs=(
            P("batch", "ctx", None),
            P("batch", "ctx", None),
            P("batch", "ctx", None),
            P(),
            P("batch", "ctx", None),
            P(),
        ),
        out_specs=(
            P("batch", "ctx", None),
            P("batch", "ctx", None),
            P("batch", "ctx", None),
            P("batch", "ctx", None),
            P(),
        ),
        check_vma=False,
    )
```

profile of v0, /device:TPU:0, one launch (start us, length us, event | category | flops | bytes accessed | tf_op | source)
XLA Modules:
  0.0 1086.7 jit_solution(6687766181752277367)
XLA Ops:
  22.7 280.8 %while.30 = (s32[]{:T(128)}, bf16[2,256,512]{2,1,0:T(8,128)(2,1)}, bf16[2,17,256,512]{3,2,0,1:T(8,128)(2,1)}, s32[]{:T(128)}, s32[]{:T(128)}, /*index=5*/s32[]{:T(128)}, s32[]{:T(128)}) while((s32[]{:T(128)}, bf16[2,256,512]{2,1,0:T(8,128)(2,1)}, bf16[2,17,256,512]{3,2,0,1:T(8,128)(2,1)}, s32[]{:T(128)}, s32[]{:T(128)}, /*index=5*/s32[]{:T(128)}, ...), condition=%wide.region_1.0_spmd, body=%wide.region_0.0_spmd.sunk | while | flops 6 | bytes 4194471 | solution.py:43
  24.7 16.6 %collective-permute-done = bf16[2,256,512]{2,1,0:T(8,128)(2,1)S(1)} collective-permute-done((bf16[2,256,512]{2,1,0:T(8,128)(2,1)}, bf16[2,256,512]{2,1,0:T(8,128)(2,1)S(1)}, u32[]{:S(2)}, u32[]{:S(2)}) %collective-permute-start) | collective-permute-done | bytes 524320 | tf_op jit(solution)/shard_map/while/body/eval_jaxpr/ppermute | solution.py:16
  42.9 16.6 %collective-permute-done = bf16[2,256,512]{2,1,0:T(8,128)(2,1)S(1)} collective-permute-done((bf16[2,256,512]{2,1,0:T(8,128)(2,1)}, bf16[2,256,512]{2,1,0:T(8,128)(2,1)S(1)}, u32[]{:S(2)}, u32[]{:S(2)}) %collective-permute-start) | collective-permute-done | bytes 524320 | tf_op jit(solution)/shard_map/while/body/eval_jaxpr/ppermute | solution.py:16
  172.5 15.9 %collective-permute-done = bf16[2,256,512]{2,1,0:T(8,128)(2,1)S(1)} collective-permute-done((bf16[2,256,512]{2,1,0:T(8,128)(2,1)}, bf16[2,256,512]{2,1,0:T(8,128)(2,1)S(1)}, u32[]{:S(2)}, u32[]{:S(2)}) %collective-permute-start) | collective-permute-done | bytes 524320 | tf_op jit(solution)/shard_map/while/body/eval_jaxpr/ppermute | solution.py:16
  190.0 17.0 %collective-permute-done = bf16[2,256,512]{2,1,0:T(8,128)(2,1)S(1)} collective-permute-done((bf16[2,256,512]{2,1,0:T(8,128)(2,1)}, bf16[2,256,512]{2,1,0:T(8,128)(2,1)S(1)}, u32[]{:S(2)}, u32[]{:S(2)}) %collective-permute-start) | collective-permute-done | bytes 524320 | tf_op jit(solution)/shard_map/while/body/eval_jaxpr/ppermute | solution.py:16
  208.6 18.1 %collective-permute-done = bf16[2,256,512]{2,1,0:T(8,128)(2,1)S(1)} collective-permute-done((bf16[2,256,512]{2,1,0:T(8,128)(2,1)}, bf16[2,256,512]{2,1,0:T(8,128)(2,1)S(1)}, u32[]{:S(2)}, u32[]{:S(2)}) %collective-permute-start) | collective-permute-done | bytes 524320 | tf_op jit(solution)/shard_map/while/body/eval_jaxpr/ppermute | solution.py:16
  228.3 19.2 %collective-permute-done = bf16[2,256,512]{2,1,0:T(8,128)(2,1)S(1)} collective-permute-done((bf16[2,256,512]{2,1,0:T(8,128)(2,1)}, bf16[2,256,512]{2,1,0:T(8,128)(2,1)S(1)}, u32[]{:S(2)}, u32[]{:S(2)}) %collective-permute-start) | collective-permute-done | bytes 524320 | tf_op jit(solution)/shard_map/while/body/eval_jaxpr/ppermute | solution.py:16
  249.1 18.4 %collective-permute-done = bf16[2,256,512]{2,1,0:T(8,128)(2,1)S(1)} collective-permute-done((bf16[2,256,512]{2,1,0:T(8,128)(2,1)}, bf16[2,256,512]{2,1,0:T(8,128)(2,1)S(1)}, u32[]{:S(2)}, u32[]{:S(2)}) %collective-permute-start) | collective-permute-done | bytes 524320 | tf_op jit(solution)/shard_map/while/body/eval_jaxpr/ppermute | solution.py:16
  269.1 17.5 %collective-permute-done = bf16[2,256,512]{2,1,0:T(8,128)(2,1)S(1)} collective-permute-done((bf16[2,256,512]{2,1,0:T(8,128)(2,1)}, bf16[2,256,512]{2,1,0:T(8,128)(2,1)S(1)}, u32[]{:S(2)}, u32[]{:S(2)}) %collective-permute-start) | collective-permute-done | bytes 524320 | tf_op jit(solution)/shard_map/while/body/eval_jaxpr/ppermute | solution.py:16
  324.9 23.1 %fusion.82 = (bf16[1,34,128,1,128]{4,3,2,1,0:T(2,128)(2,1)S(1)}, bf16[1,34,128,1,128]{4,3,2,1,0:T(2,128)(2,1)}, bf16[1,34,128,1,128]{4,3,2,1,0:T(2,128)(2,1)}, b...) fusion(bf16[2,34,128,4,128]{4,3,2,1,0:T(4,128)(2,1)} %reshape.174), kind=kLoop, calls=%fused_computation.196 | loop fusion | bytes 17825792 | tf_op jit(solution)/shard_map/slice | solution.py:59
  522.3 63.8 %psum.7 = f32[4,4]{1,0:T(4,128)S(1)} all-reduce(f32[4,4]{1,0:T(4,128)S(1)} %pad_maximum_fusion.3), channel_id=1, replica_groups=mesh['ctx'=32,'batch'=4] {'ctx','batch'}, use_global_device_ids=true, to_apply=%region_20.22 | all-reduce | flops 16 | bytes 128 | tf_op jit(solution)/shard_map/psum | solution.py:116
  621.6 20.0 %copy.128 = f32[17,2,2,128,4,128]{5,4,3,2,1,0:T(4,128)} copy(f32[17,2,2,128,4,128]{5,3,2,0,1,4:T(8,128)S(1)} %bitcast.371) | data formatting | bytes 35651584 | tf_op jit(solution)/shard_map/transpose | solution.py:104
  641.6 21.9 %reshape.183 = f32[17,2,256,512]{3,2,1,0:T(8,128)} reshape(f32[17,2,2,128,4,128]{5,4,3,2,1,0:T(4,128)} %copy.128) | data formatting | bytes 35651584 | tf_op jit(solution)/shard_map/reshape | solution.py:104
  665.9 406.7 %while.31 = (s32[]{:T(128)}, f32[2,256,512]{2,1,0:T(8,128)S(1)}, f32[17,2,256,512]{3,2,1,0:T(8,128)}, s32[]{:T(128)}, s32[]{:T(128)}, /*index=5*/s32[]{:T(128)}) while((s32[]{:T(128)}, f32[2,256,512]{2,1,0:T(8,128)S(1)}, f32[17,2,256,512]{3,2,1,0:T(8,128)}, s32[]{:T(128)}, s32[]{:T(128)}, /*index=5*/s32[]{:T(128)}) %tuple.109), condition=%wide.region_15.17_spmd, body=%wide.region_14.16_spmd.sunk | while | flops 262149 | bytes 7340179 | solution.py:110
  666.8 23.6 %collective-permute-done.1 = f32[2,256,512]{2,1,0:T(8,128)S(1)} collective-permute-done((f32[2,256,512]{2,1,0:T(8,128)S(1)}, f32[2,256,512]{2,1,0:T(8,128)S(1)}, u32[]{:S(2)}, u32[]{:S(2)}) %collective-permute-start.1) | collective-permute-done | bytes 1048608 | tf_op jit(solution)/shard_map/while/body/eval_jaxpr/ppermute | solution.py:16
  697.9 22.1 %collective-permute-done.1 = f32[2,256,512]{2,1,0:T(8,128)S(1)} collective-permute-done((f32[2,256,512]{2,1,0:T(8,128)S(1)}, f32[2,256,512]{2,1,0:T(8,128)S(1)}, u32[]{:S(2)}, u32[]{:S(2)}) %collective-permute-start.1) | collective-permute-done | bytes 1048608 | tf_op jit(solution)/shard_map/while/body/eval_jaxpr/ppermute | solution.py:16
  728.2 21.2 %collective-permute-done.1 = f32[2,256,512]{2,1,0:T(8,128)S(1)} collective-permute-done((f32[2,256,512]{2,1,0:T(8,128)S(1)}, f32[2,256,512]{2,1,0:T(8,128)S(1)}, u32[]{:S(2)}, u32[]{:S(2)}) %collective-permute-start.1) | collective-permute-done | bytes 1048608 | tf_op jit(solution)/shard_map/while/body/eval_jaxpr/ppermute | solution.py:16
  757.5 20.2 %collective-permute-done.1 = f32[2,256,512]{2,1,0:T(8,128)S(1)} collective-permute-done((f32[2,256,512]{2,1,0:T(8,128)S(1)}, f32[2,256,512]{2,1,0:T(8,128)S(1)}, u32[]{:S(2)}, u32[]{:S(2)}) %collective-permute-start.1) | collective-permute-done | bytes 1048608 | tf_op jit(solution)/shard_map/while/body/eval_jaxpr/ppermute | solution.py:16
  786.0 19.3 %collective-permute-done.1 = f32[2,256,512]{2,1,0:T(8,128)S(1)} collective-permute-done((f32[2,256,512]{2,1,0:T(8,128)S(1)}, f32[2,256,512]{2,1,0:T(8,128)S(1)}, u32[]{:S(2)}, u32[]{:S(2)}) %collective-permute-start.1) | collective-permute-done | bytes 1048608 | tf_op jit(solution)/shard_map/while/body/eval_jaxpr/ppermute | solution.py:16
  813.5 18.4 %collective-permute-done.1 = f32[2,256,512]{2,1,0:T(8,128)S(1)} collective-permute-done((f32[2,256,512]{2,1,0:T(8,128)S(1)}, f32[2,256,512]{2,1,0:T(8,128)S(1)}, u32[]{:S(2)}, u32[]{:S(2)}) %collective-permute-start.1) | collective-permute-done | bytes 1048608 | tf_op jit(solution)/shard_map/while/body/eval_jaxpr/ppermute | solution.py:16
  840.1 17.5 %collective-permute-done.1 = f32[2,256,512]{2,1,0:T(8,128)S(1)} collective-permute-done((f32[2,256,512]{2,1,0:T(8,128)S(1)}, f32[2,256,512]{2,1,0:T(8,128)S(1)}, u32[]{:S(2)}, u32[]{:S(2)}) %collective-permute-start.1) | collective-permute-done | bytes 1048608 | tf_op jit(solution)/shard_map/while/body/eval_jaxpr/ppermute | solution.py:16
  865.8 16.5 %collective-permute-done.1 = f32[2,256,512]{2,1,0:T(8,128)S(1)} collective-permute-done((f32[2,256,512]{2,1,0:T(8,128)S(1)}, f32[2,256,512]{2,1,0:T(8,128)S(1)}, u32[]{:S(2)}, u32[]{:S(2)}) %collective-permute-start.1) | collective-permute-done | bytes 1048608 | tf_op jit(solution)/shard_map/while/body/eval_jaxpr/ppermute | solution.py:16
  1008.1 16.6 %collective-permute-done.1 = f32[2,256,512]{2,1,0:T(8,128)S(1)} collective-permute-done((f32[2,256,512]{2,1,0:T(8,128)S(1)}, f32[2,256,512]{2,1,0:T(8,128)S(1)}, u32[]{:S(2)}, u32[]{:S(2)}) %collective-permute-start.1) | collective-permute-done | bytes 1048608 | tf_op jit(solution)/shard_map/while/body/eval_jaxpr/ppermute | solution.py:16
  1032.9 17.7 %collective-permute-done.1 = f32[2,256,512]{2,1,0:T(8,128)S(1)} collective-permute-done((f32[2,256,512]{2,1,0:T(8,128)S(1)}, f32[2,256,512]{2,1,0:T(8,128)S(1)}, u32[]{:S(2)}, u32[]{:S(2)}) %collective-permute-start.1) | collective-permute-done | bytes 1048608 | tf_op jit(solution)/shard_map/while/body/eval_jaxpr/ppermute | solution.py:16
  (329 shorter events, 623.7 us)
Async XLA Ops:
  22.7 18.5 %collective-permute-start = (bf16[2,256,512]{2,1,0:T(8,128)(2,1)}, bf16[2,256,512]{2,1,0:T(8,128)(2,1)S(1)}, u32[]{:S(2)}, u32[]{:S(2)}) collective-permute-start(bf16[2,256,512]{2,1,0:T(8,128)(2,1)} %get-tuple-element.288), channel_id=1, source_target_pairs={{124,0},{0,4},{4,8},{8,12},{12,16},{16,20},{20,24},{24,28},{28,32}... | collective-permute-start | bytes 1572872 | tf_op jit(solution)/shard_map/while/body/eval_jaxpr/ppermute | solution.py:16
  42.9 16.6 %collective-permute-start = (bf16[2,256,512]{2,1,0:T(8,128)(2,1)}, bf16[2,256,512]{2,1,0:T(8,128)(2,1)S(1)}, u32[]{:S(2)}, u32[]{:S(2)}) collective-permute-start(bf16[2,256,512]{2,1,0:T(8,128)(2,1)} %get-tuple-element.288), channel_id=1, source_target_pairs={{124,0},{0,4},{4,8},{8,12},{12,16},{16,20},{20,24},{24,28},{28,32}... | collective-permute-start | bytes 1572872 | tf_op jit(solution)/shard_map/while/body/eval_jaxpr/ppermute | solution.py:16
  172.5 15.9 %collective-permute-start = (bf16[2,256,512]{2,1,0:T(8,128)(2,1)}, bf16[2,256,512]{2,1,0:T(8,128)(2,1)S(1)}, u32[]{:S(2)}, u32[]{:S(2)}) collective-permute-start(bf16[2,256,512]{2,1,0:T(8,128)(2,1)} %get-tuple-element.288), channel_id=1, source_target_pairs={{124,0},{0,4},{4,8},{8,12},{12,16},{16,20},{20,24},{24,28},{28,32}... | collective-permute-start | bytes 1572872 | tf_op jit(solution)/shard_map/while/body/eval_jaxpr/ppermute | solution.py:16
  190.0 17.0 %collective-permute-start = (bf16[2,256,512]{2,1,0:T(8,128)(2,1)}, bf16[2,256,512]{2,1,0:T(8,128)(2,1)S(1)}, u32[]{:S(2)}, u32[]{:S(2)}) collective-permute-start(bf16[2,256,512]{2,1,0:T(8,128)(2,1)} %get-tuple-element.288), channel_id=1, source_target_pairs={{124,0},{0,4},{4,8},{8,12},{12,16},{16,20},{20,24},{24,28},{28,32}... | collective-permute-start | bytes 1572872 | tf_op jit(solution)/shard_map/while/body/eval_jaxpr/ppermute | solution.py:16
  208.6 18.1 %collective-permute-start = (bf16[2,256,512]{2,1,0:T(8,128)(2,1)}, bf16[2,256,512]{2,1,0:T(8,128)(2,1)S(1)}, u32[]{:S(2)}, u32[]{:S(2)}) collective-permute-start(bf16[2,256,512]{2,1,0:T(8,128)(2,1)} %get-tuple-element.288), channel_id=1, source_target_pairs={{124,0},{0,4},{4,8},{8,12},{12,16},{16,20},{20,24},{24,28},{28,32}... | collective-permute-start | bytes 1572872 | tf_op jit(solution)/shard_map/while/body/eval_jaxpr/ppermute | solution.py:16
  228.3 19.2 %collective-permute-start = (bf16[2,256,512]{2,1,0:T(8,128)(2,1)}, bf16[2,256,512]{2,1,0:T(8,128)(2,1)S(1)}, u32[]{:S(2)}, u32[]{:S(2)}) collective-permute-start(bf16[2,256,512]{2,1,0:T(8,128)(2,1)} %get-tuple-element.288), channel_id=1, source_target_pairs={{124,0},{0,4},{4,8},{8,12},{12,16},{16,20},{20,24},{24,28},{28,32}... | collective-permute-start | bytes 1572872 | tf_op jit(solution)/shard_map/while/body/eval_jaxpr/ppermute | solution.py:16
  249.1 18.4 %collective-permute-start = (bf16[2,256,512]{2,1,0:T(8,128)(2,1)}, bf16[2,256,512]{2,1,0:T(8,128)(2,1)S(1)}, u32[]{:S(2)}, u32[]{:S(2)}) collective-permute-start(bf16[2,256,512]{2,1,0:T(8,128)(2,1)} %get-tuple-element.288), channel_id=1, source_target_pairs={{124,0},{0,4},{4,8},{8,12},{12,16},{16,20},{20,24},{24,28},{28,32}... | collective-permute-start | bytes 1572872 | tf_op jit(solution)/shard_map/while/body/eval_jaxpr/ppermute | solution.py:16
  269.1 17.5 %collective-permute-start = (bf16[2,256,512]{2,1,0:T(8,128)(2,1)}, bf16[2,256,512]{2,1,0:T(8,128)(2,1)S(1)}, u32[]{:S(2)}, u32[]{:S(2)}) collective-permute-start(bf16[2,256,512]{2,1,0:T(8,128)(2,1)} %get-tuple-element.288), channel_id=1, source_target_pairs={{124,0},{0,4},{4,8},{8,12},{12,16},{16,20},{20,24},{24,28},{28,32}... | collective-permute-start | bytes 1572872 | tf_op jit(solution)/shard_map/while/body/eval_jaxpr/ppermute | solution.py:16
  665.9 24.6 %collective-permute-start.1 = (f32[2,256,512]{2,1,0:T(8,128)S(1)}, f32[2,256,512]{2,1,0:T(8,128)S(1)}, u32[]{:S(2)}, u32[]{:S(2)}) collective-permute-start(f32[2,256,512]{2,1,0:T(8,128)S(1)} %get-tuple-element.308), channel_id=1, source_target_pairs={{4,0},{8,4},{12,8},{16,12},{20,16},{24,20},{28,24},{32,28},{36,32}... | collective-permute-start | bytes 3145736 | tf_op jit(solution)/shard_map/while/body/eval_jaxpr/ppermute | solution.py:16
  691.9 28.1 %collective-permute-start.1 = (f32[2,256,512]{2,1,0:T(8,128)S(1)}, f32[2,256,512]{2,1,0:T(8,128)S(1)}, u32[]{:S(2)}, u32[]{:S(2)}) collective-permute-start(f32[2,256,512]{2,1,0:T(8,128)S(1)} %get-tuple-element.308), channel_id=1, source_target_pairs={{4,0},{8,4},{12,8},{16,12},{20,16},{24,20},{28,24},{32,28},{36,32}... | collective-permute-start | bytes 3145736 | tf_op jit(solution)/shard_map/while/body/eval_jaxpr/ppermute | solution.py:16
  721.4 27.9 %collective-permute-start.1 = (f32[2,256,512]{2,1,0:T(8,128)S(1)}, f32[2,256,512]{2,1,0:T(8,128)S(1)}, u32[]{:S(2)}, u32[]{:S(2)}) collective-permute-start(f32[2,256,512]{2,1,0:T(8,128)S(1)} %get-tuple-element.308), channel_id=1, source_target_pairs={{4,0},{8,4},{12,8},{16,12},{20,16},{24,20},{28,24},{32,28},{36,32}... | collective-permute-start | bytes 3145736 | tf_op jit(solution)/shard_map/while/body/eval_jaxpr/ppermute | solution.py:16
  750.8 27.0 %collective-permute-start.1 = (f32[2,256,512]{2,1,0:T(8,128)S(1)}, f32[2,256,512]{2,1,0:T(8,128)S(1)}, u32[]{:S(2)}, u32[]{:S(2)}) collective-permute-start(f32[2,256,512]{2,1,0:T(8,128)S(1)} %get-tuple-element.308), channel_id=1, source_target_pairs={{4,0},{8,4},{12,8},{16,12},{20,16},{24,20},{28,24},{32,28},{36,32}... | collective-permute-start | bytes 3145736 | tf_op jit(solution)/shard_map/while/body/eval_jaxpr/ppermute | solution.py:16
  779.2 26.1 %collective-permute-start.1 = (f32[2,256,512]{2,1,0:T(8,128)S(1)}, f32[2,256,512]{2,1,0:T(8,128)S(1)}, u32[]{:S(2)}, u32[]{:S(2)}) collective-permute-start(f32[2,256,512]{2,1,0:T(8,128)S(1)} %get-tuple-element.308), channel_id=1, source_target_pairs={{4,0},{8,4},{12,8},{16,12},{20,16},{24,20},{28,24},{32,28},{36,32}... | collective-permute-start | bytes 3145736 | tf_op jit(solution)/shard_map/while/body/eval_jaxpr/ppermute | solution.py:16
  806.7 25.2 %collective-permute-start.1 = (f32[2,256,512]{2,1,0:T(8,128)S(1)}, f32[2,256,512]{2,1,0:T(8,128)S(1)}, u32[]{:S(2)}, u32[]{:S(2)}) collective-permute-start(f32[2,256,512]{2,1,0:T(8,128)S(1)} %get-tuple-element.308), channel_id=1, source_target_pairs={{4,0},{8,4},{12,8},{16,12},{20,16},{24,20},{28,24},{32,28},{36,32}... | collective-permute-start | bytes 3145736 | tf_op jit(solution)/shard_map/while/body/eval_jaxpr/ppermute | solution.py:16
  833.3 24.2 %collective-permute-start.1 = (f32[2,256,512]{2,1,0:T(8,128)S(1)}, f32[2,256,512]{2,1,0:T(8,128)S(1)}, u32[]{:S(2)}, u32[]{:S(2)}) collective-permute-start(f32[2,256,512]{2,1,0:T(8,128)S(1)} %get-tuple-element.308), channel_id=1, source_target_pairs={{4,0},{8,4},{12,8},{16,12},{20,16},{24,20},{28,24},{32,28},{36,32}... | collective-permute-start | bytes 3145736 | tf_op jit(solution)/shard_map/while/body/eval_jaxpr/ppermute | solution.py:16
  859.0 23.3 %collective-permute-start.1 = (f32[2,256,512]{2,1,0:T(8,128)S(1)}, f32[2,256,512]{2,1,0:T(8,128)S(1)}, u32[]{:S(2)}, u32[]{:S(2)}) collective-permute-start(f32[2,256,512]{2,1,0:T(8,128)S(1)} %get-tuple-element.308), channel_id=1, source_target_pairs={{4,0},{8,4},{12,8},{16,12},{20,16},{24,20},{28,24},{32,28},{36,32}... | collective-permute-start | bytes 3145736 | tf_op jit(solution)/shard_map/while/body/eval_jaxpr/ppermute | solution.py:16
  883.8 22.4 %collective-permute-start.1 = (f32[2,256,512]{2,1,0:T(8,128)S(1)}, f32[2,256,512]{2,1,0:T(8,128)S(1)}, u32[]{:S(2)}, u32[]{:S(2)}) collective-permute-start(f32[2,256,512]{2,1,0:T(8,128)S(1)} %get-tuple-element.308), channel_id=1, source_target_pairs={{4,0},{8,4},{12,8},{16,12},{20,16},{24,20},{28,24},{32,28},{36,32}... | collective-permute-start | bytes 3145736 | tf_op jit(solution)/shard_map/while/body/eval_jaxpr/ppermute | solution.py:16
  907.6 21.9 %collective-permute-start.1 = (f32[2,256,512]{2,1,0:T(8,128)S(1)}, f32[2,256,512]{2,1,0:T(8,128)S(1)}, u32[]{:S(2)}, u32[]{:S(2)}) collective-permute-start(f32[2,256,512]{2,1,0:T(8,128)S(1)} %get-tuple-element.308), channel_id=1, source_target_pairs={{4,0},{8,4},{12,8},{16,12},{20,16},{24,20},{28,24},{32,28},{36,32}... | collective-permute-start | bytes 3145736 | tf_op jit(solution)/shard_map/while/body/eval_jaxpr/ppermute | solution.py:16
  930.9 21.9 %collective-permute-start.1 = (f32[2,256,512]{2,1,0:T(8,128)S(1)}, f32[2,256,512]{2,1,0:T(8,128)S(1)}, u32[]{:S(2)}, u32[]{:S(2)}) collective-permute-start(f32[2,256,512]{2,1,0:T(8,128)S(1)} %get-tuple-element.308), channel_id=1, source_target_pairs={{4,0},{8,4},{12,8},{16,12},{20,16},{24,20},{28,24},{32,28},{36,32}... | collective-permute-start | bytes 3145736 | tf_op jit(solution)/shard_map/while/body/eval_jaxpr/ppermute | solution.py:16
  954.3 21.9 %collective-permute-start.1 = (f32[2,256,512]{2,1,0:T(8,128)S(1)}, f32[2,256,512]{2,1,0:T(8,128)S(1)}, u32[]{:S(2)}, u32[]{:S(2)}) collective-permute-start(f32[2,256,512]{2,1,0:T(8,128)S(1)} %get-tuple-element.308), channel_id=1, source_target_pairs={{4,0},{8,4},{12,8},{16,12},{20,16},{24,20},{28,24},{32,28},{36,32}... | collective-permute-start | bytes 3145736 | tf_op jit(solution)/shard_map/while/body/eval_jaxpr/ppermute | solution.py:16
  977.6 22.3 %collective-permute-start.1 = (f32[2,256,512]{2,1,0:T(8,128)S(1)}, f32[2,256,512]{2,1,0:T(8,128)S(1)}, u32[]{:S(2)}, u32[]{:S(2)}) collective-permute-start(f32[2,256,512]{2,1,0:T(8,128)S(1)} %get-tuple-element.308), channel_id=1, source_target_pairs={{4,0},{8,4},{12,8},{16,12},{20,16},{24,20},{28,24},{32,28},{36,32}... | collective-permute-start | bytes 3145736 | tf_op jit(solution)/shard_map/while/body/eval_jaxpr/ppermute | solution.py:16
  1001.3 23.4 %collective-permute-start.1 = (f32[2,256,512]{2,1,0:T(8,128)S(1)}, f32[2,256,512]{2,1,0:T(8,128)S(1)}, u32[]{:S(2)}, u32[]{:S(2)}) collective-permute-start(f32[2,256,512]{2,1,0:T(8,128)S(1)} %get-tuple-element.308), channel_id=1, source_target_pairs={{4,0},{8,4},{12,8},{16,12},{20,16},{24,20},{28,24},{32,28},{36,32}... | collective-permute-start | bytes 3145736 | tf_op jit(solution)/shard_map/while/body/eval_jaxpr/ppermute | solution.py:16
  1026.1 24.5 %collective-permute-start.1 = (f32[2,256,512]{2,1,0:T(8,128)S(1)}, f32[2,256,512]{2,1,0:T(8,128)S(1)}, u32[]{:S(2)}, u32[]{:S(2)}) collective-permute-start(f32[2,256,512]{2,1,0:T(8,128)S(1)} %get-tuple-element.308), channel_id=1, source_target_pairs={{4,0},{8,4},{12,8},{16,12},{20,16},{24,20},{28,24},{32,28},{36,32}... | collective-permute-start | bytes 3145736 | tf_op jit(solution)/shard_map/while/body/eval_jaxpr/ppermute | solution.py:16
  1052.0 19.1 %collective-permute-start.1 = (f32[2,256,512]{2,1,0:T(8,128)S(1)}, f32[2,256,512]{2,1,0:T(8,128)S(1)}, u32[]{:S(2)}, u32[]{:S(2)}) collective-permute-start(f32[2,256,512]{2,1,0:T(8,128)S(1)} %get-tuple-element.308), channel_id=1, source_target_pairs={{4,0},{8,4},{12,8},{16,12},{20,16},{24,20},{28,24},{32,28},{36,32}... | collective-permute-start | bytes 3145736 | tf_op jit(solution)/shard_map/while/body/eval_jaxpr/ppermute | solution.py:16
  (60 other events, 414.3 us)
where the time goes:
time: 1100 us; the launch traced here: 1090 us
  waiting for transfers between devices  536 us (49%)
  local copies, waits for them, and re-layouts  211 us (19%)
  matrix products  114 us (10%)
  starting transfers between devices  107 us (10%)
  blocking collectives  63.8 us (6%)
  other arithmetic  52.3 us (5%)
    ppermute x34, waiting for transfers between devices, passed_along(): return lax.ppermute(block, axis, route)  536 us
    ppermute x34, starting transfers between devices, passed_along(): return lax.ppermute(block, axis, route)  107 us
    psum x1, blocking collectives, body(): scale_total = lax.psum(jnp.stack(scale_parts), ('ctx', 'batch'))  63.8 us
    another operation x6, local copies, waits for them, and re-layouts, body(): jnp.stack(placed_parts)  24.6 us
    dot_general x4, matrix products, body(): jnp.einsum('sw,csx->cwx', chooser, both_parts, precision=lax.Precision.HI...  24.4 us
    slice x1, local copies, waits for them, and re-layouts, body(): blocks_all[0, :, :, group_id]  23.1 us
    add x16, other arithmetic, chain_turn(): moved + lax.dynamic_index_in_dim(grads_window, turn_no, 0, keepdims=False)  22.9 us
  transfers between devices with their start and end apart: 34, of which 34 were waited for; matrix products, arithmetic and copies ran while one was open for 2% of the time, Pallas kernels for 0%

commit v1 on v0

--- a/solution.py
+++ b/solution.py
@@ -113,7 +113,7 @@
     )
     key_grad = summed[0].reshape(1, tokens, KV_HEADS * HD).astype(jnp.bfloat16)
     value_grad = summed[1].reshape(1, tokens, KV_HEADS * HD).astype(jnp.bfloat16)
-    scale_total = lax.psum(jnp.stack(scale_parts), ("ctx", "batch"))
+    scale_total = lax.psum(lax.psum(jnp.stack(scale_parts), "batch"), "ctx")
     tau_grad = scale_total.reshape(HEADS) / math.sqrt(lax.axis_size("batch") * ctx_size * tokens)
     return (attended, query_grad, key_grad, value_grad, tau_grad)
 

time: 1100 us -> 1140 us (1.036)
  waiting for transfers between devices: 536 us -> 576 us
  blocking collectives: 63.8 us -> 84.2 us
  starting transfers between devices: 107 us -> 95.1 us
    ppermute x34, waiting for transfers between devices: 536 us -> 576 us  [passed_along(): return lax.ppermute(block, axis, route)]
    psum x1 -> x2, blocking collectives: 63.8 us -> 84.2 us  [body(): scale_total = lax.psum(lax.psum(jnp.stack(scale_parts), 'batch'), 'ctx')]
    ppermute x34, starting transfers between devices: 107 us -> 95.1 us  [passed_along(): return lax.ppermute(block, axis, route)]
where the time goes in v1:
time: 1140 us; the launch traced here: 1130 us
  waiting for transfers between devices  576 us (51%)
  local copies, waits for them, and re-layouts  212 us (19%)
  matrix products  115 us (10%)
  starting transfers between devices  95.1 us (8%)
  blocking collectives  84.2 us (7%)
  other arithmetic  50.9 us (4%)
    ppermute x34, waiting for transfers between devices, passed_along(): return lax.ppermute(block, axis, route)  576 us
    ppermute x34, starting transfers between devices, passed_along(): return lax.ppermute(block, axis, route)  95.1 us
    psum x2, blocking collectives, body(): scale_total = lax.psum(lax.psum(jnp.stack(scale_parts), 'batch'), 'ctx')  84.2 us
    dot_general x4, matrix products, body(): jnp.einsum('sw,csx->cwx', chooser, both_parts, precision=lax.Precision.HI...  25.9 us
    another operation x6, local copies, waits for them, and re-layouts, body(): jnp.stack(placed_parts)  24.5 us
    slice x1, local copies, waits for them, and re-layouts, body(): blocks_all[0, :, :, group_id]  23.5 us
    add x16, other arithmetic, chain_turn(): moved + lax.dynamic_index_in_dim(grads_window, turn_no, 0, keepdims=False)  22.9 us
  transfers between devices with their start and end apart: 34, of which 34 were waited for; matrix products, arithmetic and copies ran while one was open for 2% of the time, Pallas kernels for 0%

profile of v1, /device:TPU:0, one launch (start us, length us, event | category | flops | bytes accessed | tf_op | source)
XLA Modules:
  0.0 1134.4 jit_solution(5244243100836570360)
XLA Ops:
  22.7 281.0 %while.30 = (s32[]{:T(128)}, bf16[2,256,512]{2,1,0:T(8,128)(2,1)}, bf16[2,17,256,512]{3,2,0,1:T(8,128)(2,1)}, s32[]{:T(128)}, s32[]{:T(128)}, /*index=5*/s32[]{:T(128)}, s32[]{:T(128)}) while((s32[]{:T(128)}, bf16[2,256,512]{2,1,0:T(8,128)(2,1)}, bf16[2,17,256,512]{3,2,0,1:T(8,128)(2,1)}, s32[]{:T(128)}, s32[]{:T(128)}, /*index=5*/s32[]{:T(128)}, ...), condition=%wide.region_1.0_spmd, body=%wide.region_0.0_spmd.sunk | while | flops 6 | bytes 4194471 | solution.py:43
  190.1 16.9 %collective-permute-done = bf16[2,256,512]{2,1,0:T(8,128)(2,1)S(1)} collective-permute-done((bf16[2,256,512]{2,1,0:T(8,128)(2,1)}, bf16[2,256,512]{2,1,0:T(8,128)(2,1)S(1)}, u32[]{:S(2)}, u32[]{:S(2)}) %collective-permute-start) | collective-permute-done | bytes 524320 | tf_op jit(solution)/shard_map/while/body/eval_jaxpr/ppermute | solution.py:16
  208.7 18.1 %collective-permute-done = bf16[2,256,512]{2,1,0:T(8,128)(2,1)S(1)} collective-permute-done((bf16[2,256,512]{2,1,0:T(8,128)(2,1)}, bf16[2,256,512]{2,1,0:T(8,128)(2,1)S(1)}, u32[]{:S(2)}, u32[]{:S(2)}) %collective-permute-start) | collective-permute-done | bytes 524320 | tf_op jit(solution)/shard_map/while/body/eval_jaxpr/ppermute | solution.py:16
  228.4 19.2 %collective-permute-done = bf16[2,256,512]{2,1,0:T(8,128)(2,1)S(1)} collective-permute-done((bf16[2,256,512]{2,1,0:T(8,128)(2,1)}, bf16[2,256,512]{2,1,0:T(8,128)(2,1)S(1)}, u32[]{:S(2)}, u32[]{:S(2)}) %collective-permute-start) | collective-permute-done | bytes 524320 | tf_op jit(solution)/shard_map/while/body/eval_jaxpr/ppermute | solution.py:16
  249.3 18.4 %collective-permute-done = bf16[2,256,512]{2,1,0:T(8,128)(2,1)S(1)} collective-permute-done((bf16[2,256,512]{2,1,0:T(8,128)(2,1)}, bf16[2,256,512]{2,1,0:T(8,128)(2,1)S(1)}, u32[]{:S(2)}, u32[]{:S(2)}) %collective-permute-start) | collective-permute-done | bytes 524320 | tf_op jit(solution)/shard_map/while/body/eval_jaxpr/ppermute | solution.py:16
  269.3 17.5 %collective-permute-done = bf16[2,256,512]{2,1,0:T(8,128)(2,1)S(1)} collective-permute-done((bf16[2,256,512]{2,1,0:T(8,128)(2,1)}, bf16[2,256,512]{2,1,0:T(8,128)(2,1)S(1)}, u32[]{:S(2)}, u32[]{:S(2)}) %collective-permute-start) | collective-permute-done | bytes 524320 | tf_op jit(solution)/shard_map/while/body/eval_jaxpr/ppermute | solution.py:16
  325.1 23.5 %fusion.82 = (bf16[1,34,128,1,128]{4,3,2,1,0:T(2,128)(2,1)S(1)}, bf16[1,34,128,1,128]{4,3,2,1,0:T(2,128)(2,1)}, bf16[1,34,128,1,128]{4,3,2,1,0:T(2,128)(2,1)}, b...) fusion(bf16[2,34,128,4,128]{4,3,2,1,0:T(4,128)(2,1)} %reshape.174), kind=kLoop, calls=%fused_computation.196 | loop fusion | bytes 17825792 | tf_op jit(solution)/shard_map/slice | solution.py:59
  530.1 77.0 %psum.15 = f32[4,4]{1,0:T(4,128)S(1)} all-reduce(f32[4,4]{1,0:T(4,128)S(1)} %psum.14), channel_id=1, replica_groups=mesh['ctx'=32,'batch'=4] {'ctx'}, use_global_device_ids=true, to_apply=%region_21.23 | all-reduce | flops 16 | bytes 128 | tf_op jit(solution)/shard_map/psum | solution.py:116
  642.4 19.9 %copy.128 = f32[17,2,2,128,4,128]{5,4,3,2,1,0:T(4,128)} copy(f32[17,2,2,128,4,128]{5,3,2,0,1,4:T(8,128)S(1)} %bitcast.371) | data formatting | bytes 35651584 | tf_op jit(solution)/shard_map/transpose | solution.py:104
  662.3 21.9 %reshape.183 = f32[17,2,256,512]{3,2,1,0:T(8,128)} reshape(f32[17,2,2,128,4,128]{5,4,3,2,1,0:T(4,128)} %copy.128) | data formatting | bytes 35651584 | tf_op jit(solution)/shard_map/reshape | solution.py:104
  686.7 433.6 %while.31 = (s32[]{:T(128)}, f32[2,256,512]{2,1,0:T(8,128)S(1)}, f32[17,2,256,512]{3,2,1,0:T(8,128)}, s32[]{:T(128)}, s32[]{:T(128)}, /*index=5*/s32[]{:T(128)}) while((s32[]{:T(128)}, f32[2,256,512]{2,1,0:T(8,128)S(1)}, f32[17,2,256,512]{3,2,1,0:T(8,128)}, s32[]{:T(128)}, s32[]{:T(128)}, /*index=5*/s32[]{:T(128)}) %tuple.109), condition=%wide.region_15.17_spmd, body=%wide.region_14.16_spmd.sunk | while | flops 262149 | bytes 7340179 | solution.py:110
  688.7 22.3 %collective-permute-done.1 = f32[2,256,512]{2,1,0:T(8,128)S(1)} collective-permute-done((f32[2,256,512]{2,1,0:T(8,128)S(1)}, f32[2,256,512]{2,1,0:T(8,128)S(1)}, u32[]{:S(2)}, u32[]{:S(2)}) %collective-permute-start.1) | collective-permute-done | bytes 1048608 | tf_op jit(solution)/shard_map/while/body/eval_jaxpr/ppermute | solution.py:16
  715.2 23.9 %collective-permute-done.1 = f32[2,256,512]{2,1,0:T(8,128)S(1)} collective-permute-done((f32[2,256,512]{2,1,0:T(8,128)S(1)}, f32[2,256,512]{2,1,0:T(8,128)S(1)}, u32[]{:S(2)}, u32[]{:S(2)}) %collective-permute-start.1) | collective-permute-done | bytes 1048608 | tf_op jit(solution)/shard_map/while/body/eval_jaxpr/ppermute | solution.py:16
  742.8 24.5 %collective-permute-done.1 = f32[2,256,512]{2,1,0:T(8,128)S(1)} collective-permute-done((f32[2,256,512]{2,1,0:T(8,128)S(1)}, f32[2,256,512]{2,1,0:T(8,128)S(1)}, u32[]{:S(2)}, u32[]{:S(2)}) %collective-permute-start.1) | collective-permute-done | bytes 1048608 | tf_op jit(solution)/shard_map/while/body/eval_jaxpr/ppermute | solution.py:16
  771.4 22.6 %collective-permute-done.1 = f32[2,256,512]{2,1,0:T(8,128)S(1)} collective-permute-done((f32[2,256,512]{2,1,0:T(8,128)S(1)}, f32[2,256,512]{2,1,0:T(8,128)S(1)}, u32[]{:S(2)}, u32[]{:S(2)}) %collective-permute-start.1) | collective-permute-done | bytes 1048608 | tf_op jit(solution)/shard_map/while/body/eval_jaxpr/ppermute | solution.py:16
  801.1 22.7 %collective-permute-done.1 = f32[2,256,512]{2,1,0:T(8,128)S(1)} collective-permute-done((f32[2,256,512]{2,1,0:T(8,128)S(1)}, f32[2,256,512]{2,1,0:T(8,128)S(1)}, u32[]{:S(2)}, u32[]{:S(2)}) %collective-permute-start.1) | collective-permute-done | bytes 1048608 | tf_op jit(solution)/shard_map/while/body/eval_jaxpr/ppermute | solution.py:16
  832.0 23.3 %collective-permute-done.1 = f32[2,256,512]{2,1,0:T(8,128)S(1)} collective-permute-done((f32[2,256,512]{2,1,0:T(8,128)S(1)}, f32[2,256,512]{2,1,0:T(8,128)S(1)}, u32[]{:S(2)}, u32[]{:S(2)}) %collective-permute-start.1) | collective-permute-done | bytes 1048608 | tf_op jit(solution)/shard_map/while/body/eval_jaxpr/ppermute | solution.py:16
  863.5 22.4 %collective-permute-done.1 = f32[2,256,512]{2,1,0:T(8,128)S(1)} collective-permute-done((f32[2,256,512]{2,1,0:T(8,128)S(1)}, f32[2,256,512]{2,1,0:T(8,128)S(1)}, u32[]{:S(2)}, u32[]{:S(2)}) %collective-permute-start.1) | collective-permute-done | bytes 1048608 | tf_op jit(solution)/shard_map/while/body/eval_jaxpr/ppermute | solution.py:16
  894.1 21.6 %collective-permute-done.1 = f32[2,256,512]{2,1,0:T(8,128)S(1)} collective-permute-done((f32[2,256,512]{2,1,0:T(8,128)S(1)}, f32[2,256,512]{2,1,0:T(8,128)S(1)}, u32[]{:S(2)}, u32[]{:S(2)}) %collective-permute-start.1) | collective-permute-done | bytes 1048608 | tf_op jit(solution)/shard_map/while/body/eval_jaxpr/ppermute | solution.py:16
  923.9 20.6 %collective-permute-done.1 = f32[2,256,512]{2,1,0:T(8,128)S(1)} collective-permute-done((f32[2,256,512]{2,1,0:T(8,128)S(1)}, f32[2,256,512]{2,1,0:T(8,128)S(1)}, u32[]{:S(2)}, u32[]{:S(2)}) %collective-permute-start.1) | collective-permute-done | bytes 1048608 | tf_op jit(solution)/shard_map/while/body/eval_jaxpr/ppermute | solution.py:16
  952.8 19.7 %collective-permute-done.1 = f32[2,256,512]{2,1,0:T(8,128)S(1)} collective-permute-done((f32[2,256,512]{2,1,0:T(8,128)S(1)}, f32[2,256,512]{2,1,0:T(8,128)S(1)}, u32[]{:S(2)}, u32[]{:S(2)}) %collective-permute-start.1) | collective-permute-done | bytes 1048608 | tf_op jit(solution)/shard_map/while/body/eval_jaxpr/ppermute | solution.py:16
  980.7 18.8 %collective-permute-done.1 = f32[2,256,512]{2,1,0:T(8,128)S(1)} collective-permute-done((f32[2,256,512]{2,1,0:T(8,128)S(1)}, f32[2,256,512]{2,1,0:T(8,128)S(1)}, u32[]{:S(2)}, u32[]{:S(2)}) %collective-permute-start.1) | collective-permute-done | bytes 1048608 | tf_op jit(solution)/shard_map/while/body/eval_jaxpr/ppermute | solution.py:16
  1007.7 17.9 %collective-permute-done.1 = f32[2,256,512]{2,1,0:T(8,128)S(1)} collective-permute-done((f32[2,256,512]{2,1,0:T(8,128)S(1)}, f32[2,256,512]{2,1,0:T(8,128)S(1)}, u32[]{:S(2)}, u32[]{:S(2)}) %collective-permute-start.1) | collective-permute-done | bytes 1048608 | tf_op jit(solution)/shard_map/while/body/eval_jaxpr/ppermute | solution.py:16
  1033.8 17.0 %collective-permute-done.1 = f32[2,256,512]{2,1,0:T(8,128)S(1)} collective-permute-done((f32[2,256,512]{2,1,0:T(8,128)S(1)}, f32[2,256,512]{2,1,0:T(8,128)S(1)}, u32[]{:S(2)}, u32[]{:S(2)}) %collective-permute-start.1) | collective-permute-done | bytes 1048608 | tf_op jit(solution)/shard_map/while/body/eval_jaxpr/ppermute | solution.py:16
  (326 shorter events, 622.8 us)
Async XLA Ops:
  22.7 18.5 %collective-permute-start = (bf16[2,256,512]{2,1,0:T(8,128)(2,1)}, bf16[2,256,512]{2,1,0:T(8,128)(2,1)S(1)}, u32[]{:S(2)}, u32[]{:S(2)}) collective-permute-start(bf16[2,256,512]{2,1,0:T(8,128)(2,1)} %get-tuple-element.288), channel_id=1, source_target_pairs={{124,0},{0,4},{4,8},{8,12},{12,16},{16,20},{20,24},{24,28},{28,32}... | collective-permute-start | bytes 1572872 | tf_op jit(solution)/shard_map/while/body/eval_jaxpr/ppermute | solution.py:16
  42.9 16.6 %collective-permute-start = (bf16[2,256,512]{2,1,0:T(8,128)(2,1)}, bf16[2,256,512]{2,1,0:T(8,128)(2,1)S(1)}, u32[]{:S(2)}, u32[]{:S(2)}) collective-permute-start(bf16[2,256,512]{2,1,0:T(8,128)(2,1)} %get-tuple-element.288), channel_id=1, source_target_pairs={{124,0},{0,4},{4,8},{8,12},{12,16},{16,20},{20,24},{24,28},{28,32}... | collective-permute-start | bytes 1572872 | tf_op jit(solution)/shard_map/while/body/eval_jaxpr/ppermute | solution.py:16
  172.6 15.8 %collective-permute-start = (bf16[2,256,512]{2,1,0:T(8,128)(2,1)}, bf16[2,256,512]{2,1,0:T(8,128)(2,1)S(1)}, u32[]{:S(2)}, u32[]{:S(2)}) collective-permute-start(bf16[2,256,512]{2,1,0:T(8,128)(2,1)} %get-tuple-element.288), channel_id=1, source_target_pairs={{124,0},{0,4},{4,8},{8,12},{12,16},{16,20},{20,24},{24,28},{28,32}... | collective-permute-start | bytes 1572872 | tf_op jit(solution)/shard_map/while/body/eval_jaxpr/ppermute | solution.py:16
  190.1 16.9 %collective-permute-start = (bf16[2,256,512]{2,1,0:T(8,128)(2,1)}, bf16[2,256,512]{2,1,0:T(8,128)(2,1)S(1)}, u32[]{:S(2)}, u32[]{:S(2)}) collective-permute-start(bf16[2,256,512]{2,1,0:T(8,128)(2,1)} %get-tuple-element.288), channel_id=1, source_target_pairs={{124,0},{0,4},{4,8},{8,12},{12,16},{16,20},{20,24},{24,28},{28,32}... | collective-permute-start | bytes 1572872 | tf_op jit(solution)/shard_map/while/body/eval_jaxpr/ppermute | solution.py:16
  208.7 18.1 %collective-permute-start = (bf16[2,256,512]{2,1,0:T(8,128)(2,1)}, bf16[2,256,512]{2,1,0:T(8,128)(2,1)S(1)}, u32[]{:S(2)}, u32[]{:S(2)}) collective-permute-start(bf16[2,256,512]{2,1,0:T(8,128)(2,1)} %get-tuple-element.288), channel_id=1, source_target_pairs={{124,0},{0,4},{4,8},{8,12},{12,16},{16,20},{20,24},{24,28},{28,32}... | collective-permute-start | bytes 1572872 | tf_op jit(solution)/shard_map/while/body/eval_jaxpr/ppermute | solution.py:16
  228.4 19.2 %collective-permute-start = (bf16[2,256,512]{2,1,0:T(8,128)(2,1)}, bf16[2,256,512]{2,1,0:T(8,128)(2,1)S(1)}, u32[]{:S(2)}, u32[]{:S(2)}) collective-permute-start(bf16[2,256,512]{2,1,0:T(8,128)(2,1)} %get-tuple-element.288), channel_id=1, source_target_pairs={{124,0},{0,4},{4,8},{8,12},{12,16},{16,20},{20,24},{24,28},{28,32}... | collective-permute-start | bytes 1572872 | tf_op jit(solution)/shard_map/while/body/eval_jaxpr/ppermute | solution.py:16
  249.3 18.4 %collective-permute-start = (bf16[2,256,512]{2,1,0:T(8,128)(2,1)}, bf16[2,256,512]{2,1,0:T(8,128)(2,1)S(1)}, u32[]{:S(2)}, u32[]{:S(2)}) collective-permute-start(bf16[2,256,512]{2,1,0:T(8,128)(2,1)} %get-tuple-element.288), channel_id=1, source_target_pairs={{124,0},{0,4},{4,8},{8,12},{12,16},{16,20},{20,24},{24,28},{28,32}... | collective-permute-start | bytes 1572872 | tf_op jit(solution)/shard_map/while/body/eval_jaxpr/ppermute | solution.py:16
  269.3 17.5 %collective-permute-start = (bf16[2,256,512]{2,1,0:T(8,128)(2,1)}, bf16[2,256,512]{2,1,0:T(8,128)(2,1)S(1)}, u32[]{:S(2)}, u32[]{:S(2)}) collective-permute-start(bf16[2,256,512]{2,1,0:T(8,128)(2,1)} %get-tuple-element.288), channel_id=1, source_target_pairs={{124,0},{0,4},{4,8},{8,12},{12,16},{16,20},{20,24},{24,28},{28,32}... | collective-permute-start | bytes 1572872 | tf_op jit(solution)/shard_map/while/body/eval_jaxpr/ppermute | solution.py:16
  686.7 24.3 %collective-permute-start.1 = (f32[2,256,512]{2,1,0:T(8,128)S(1)}, f32[2,256,512]{2,1,0:T(8,128)S(1)}, u32[]{:S(2)}, u32[]{:S(2)}) collective-permute-start(f32[2,256,512]{2,1,0:T(8,128)S(1)} %get-tuple-element.308), channel_id=1, source_target_pairs={{4,0},{8,4},{12,8},{16,12},{20,16},{24,20},{28,24},{32,28},{36,32}... | collective-permute-start | bytes 3145736 | tf_op jit(solution)/shard_map/while/body/eval_jaxpr/ppermute | solution.py:16
  712.4 26.6 %collective-permute-start.1 = (f32[2,256,512]{2,1,0:T(8,128)S(1)}, f32[2,256,512]{2,1,0:T(8,128)S(1)}, u32[]{:S(2)}, u32[]{:S(2)}) collective-permute-start(f32[2,256,512]{2,1,0:T(8,128)S(1)} %get-tuple-element.308), channel_id=1, source_target_pairs={{4,0},{8,4},{12,8},{16,12},{20,16},{24,20},{28,24},{32,28},{36,32}... | collective-permute-start | bytes 3145736 | tf_op jit(solution)/shard_map/while/body/eval_jaxpr/ppermute | solution.py:16
  740.5 26.8 %collective-permute-start.1 = (f32[2,256,512]{2,1,0:T(8,128)S(1)}, f32[2,256,512]{2,1,0:T(8,128)S(1)}, u32[]{:S(2)}, u32[]{:S(2)}) collective-permute-start(f32[2,256,512]{2,1,0:T(8,128)S(1)} %get-tuple-element.308), channel_id=1, source_target_pairs={{4,0},{8,4},{12,8},{16,12},{20,16},{24,20},{28,24},{32,28},{36,32}... | collective-permute-start | bytes 3145736 | tf_op jit(solution)/shard_map/while/body/eval_jaxpr/ppermute | solution.py:16
  768.7 25.3 %collective-permute-start.1 = (f32[2,256,512]{2,1,0:T(8,128)S(1)}, f32[2,256,512]{2,1,0:T(8,128)S(1)}, u32[]{:S(2)}, u32[]{:S(2)}) collective-permute-start(f32[2,256,512]{2,1,0:T(8,128)S(1)} %get-tuple-element.308), channel_id=1, source_target_pairs={{4,0},{8,4},{12,8},{16,12},{20,16},{24,20},{28,24},{32,28},{36,32}... | collective-permute-start | bytes 3145736 | tf_op jit(solution)/shard_map/while/body/eval_jaxpr/ppermute | solution.py:16
  795.5 28.3 %collective-permute-start.1 = (f32[2,256,512]{2,1,0:T(8,128)S(1)}, f32[2,256,512]{2,1,0:T(8,128)S(1)}, u32[]{:S(2)}, u32[]{:S(2)}) collective-permute-start(f32[2,256,512]{2,1,0:T(8,128)S(1)} %get-tuple-element.308), channel_id=1, source_target_pairs={{4,0},{8,4},{12,8},{16,12},{20,16},{24,20},{28,24},{32,28},{36,32}... | collective-permute-start | bytes 3145736 | tf_op jit(solution)/shard_map/while/body/eval_jaxpr/ppermute | solution.py:16
  825.2 30.1 %collective-permute-start.1 = (f32[2,256,512]{2,1,0:T(8,128)S(1)}, f32[2,256,512]{2,1,0:T(8,128)S(1)}, u32[]{:S(2)}, u32[]{:S(2)}) collective-permute-start(f32[2,256,512]{2,1,0:T(8,128)S(1)} %get-tuple-element.308), channel_id=1, source_target_pairs={{4,0},{8,4},{12,8},{16,12},{20,16},{24,20},{28,24},{32,28},{36,32}... | collective-permute-start | bytes 3145736 | tf_op jit(solution)/shard_map/while/body/eval_jaxpr/ppermute | solution.py:16
  856.7 29.2 %collective-permute-start.1 = (f32[2,256,512]{2,1,0:T(8,128)S(1)}, f32[2,256,512]{2,1,0:T(8,128)S(1)}, u32[]{:S(2)}, u32[]{:S(2)}) collective-permute-start(f32[2,256,512]{2,1,0:T(8,128)S(1)} %get-tuple-element.308), channel_id=1, source_target_pairs={{4,0},{8,4},{12,8},{16,12},{20,16},{24,20},{28,24},{32,28},{36,32}... | collective-permute-start | bytes 3145736 | tf_op jit(solution)/shard_map/while/body/eval_jaxpr/ppermute | solution.py:16
  887.4 28.3 %collective-permute-start.1 = (f32[2,256,512]{2,1,0:T(8,128)S(1)}, f32[2,256,512]{2,1,0:T(8,128)S(1)}, u32[]{:S(2)}, u32[]{:S(2)}) collective-permute-start(f32[2,256,512]{2,1,0:T(8,128)S(1)} %get-tuple-element.308), channel_id=1, source_target_pairs={{4,0},{8,4},{12,8},{16,12},{20,16},{24,20},{28,24},{32,28},{36,32}... | collective-permute-start | bytes 3145736 | tf_op jit(solution)/shard_map/while/body/eval_jaxpr/ppermute | solution.py:16
  917.1 27.4 %collective-permute-start.1 = (f32[2,256,512]{2,1,0:T(8,128)S(1)}, f32[2,256,512]{2,1,0:T(8,128)S(1)}, u32[]{:S(2)}, u32[]{:S(2)}) collective-permute-start(f32[2,256,512]{2,1,0:T(8,128)S(1)} %get-tuple-element.308), channel_id=1, source_target_pairs={{4,0},{8,4},{12,8},{16,12},{20,16},{24,20},{28,24},{32,28},{36,32}... | collective-permute-start | bytes 3145736 | tf_op jit(solution)/shard_map/while/body/eval_jaxpr/ppermute | solution.py:16
  946.0 26.5 %collective-permute-start.1 = (f32[2,256,512]{2,1,0:T(8,128)S(1)}, f32[2,256,512]{2,1,0:T(8,128)S(1)}, u32[]{:S(2)}, u32[]{:S(2)}) collective-permute-start(f32[2,256,512]{2,1,0:T(8,128)S(1)} %get-tuple-element.308), channel_id=1, source_target_pairs={{4,0},{8,4},{12,8},{16,12},{20,16},{24,20},{28,24},{32,28},{36,32}... | collective-permute-start | bytes 3145736 | tf_op jit(solution)/shard_map/while/body/eval_jaxpr/ppermute | solution.py:16
  973.9 25.6 %collective-permute-start.1 = (f32[2,256,512]{2,1,0:T(8,128)S(1)}, f32[2,256,512]{2,1,0:T(8,128)S(1)}, u32[]{:S(2)}, u32[]{:S(2)}) collective-permute-start(f32[2,256,512]{2,1,0:T(8,128)S(1)} %get-tuple-element.308), channel_id=1, source_target_pairs={{4,0},{8,4},{12,8},{16,12},{20,16},{24,20},{28,24},{32,28},{36,32}... | collective-permute-start | bytes 3145736 | tf_op jit(solution)/shard_map/while/body/eval_jaxpr/ppermute | solution.py:16
  1000.9 24.6 %collective-permute-start.1 = (f32[2,256,512]{2,1,0:T(8,128)S(1)}, f32[2,256,512]{2,1,0:T(8,128)S(1)}, u32[]{:S(2)}, u32[]{:S(2)}) collective-permute-start(f32[2,256,512]{2,1,0:T(8,128)S(1)} %get-tuple-element.308), channel_id=1, source_target_pairs={{4,0},{8,4},{12,8},{16,12},{20,16},{24,20},{28,24},{32,28},{36,32}... | collective-permute-start | bytes 3145736 | tf_op jit(solution)/shard_map/while/body/eval_jaxpr/ppermute | solution.py:16
  1027.0 23.7 %collective-permute-start.1 = (f32[2,256,512]{2,1,0:T(8,128)S(1)}, f32[2,256,512]{2,1,0:T(8,128)S(1)}, u32[]{:S(2)}, u32[]{:S(2)}) collective-permute-start(f32[2,256,512]{2,1,0:T(8,128)S(1)} %get-tuple-element.308), channel_id=1, source_target_pairs={{4,0},{8,4},{12,8},{16,12},{20,16},{24,20},{28,24},{32,28},{36,32}... | collective-permute-start | bytes 3145736 | tf_op jit(solution)/shard_map/while/body/eval_jaxpr/ppermute | solution.py:16
  1052.2 22.8 %collective-permute-start.1 = (f32[2,256,512]{2,1,0:T(8,128)S(1)}, f32[2,256,512]{2,1,0:T(8,128)S(1)}, u32[]{:S(2)}, u32[]{:S(2)}) collective-permute-start(f32[2,256,512]{2,1,0:T(8,128)S(1)} %get-tuple-element.308), channel_id=1, source_target_pairs={{4,0},{8,4},{12,8},{16,12},{20,16},{24,20},{28,24},{32,28},{36,32}... | collective-permute-start | bytes 3145736 | tf_op jit(solution)/shard_map/while/body/eval_jaxpr/ppermute | solution.py:16
  1076.5 21.9 %collective-permute-start.1 = (f32[2,256,512]{2,1,0:T(8,128)S(1)}, f32[2,256,512]{2,1,0:T(8,128)S(1)}, u32[]{:S(2)}, u32[]{:S(2)}) collective-permute-start(f32[2,256,512]{2,1,0:T(8,128)S(1)} %get-tuple-element.308), channel_id=1, source_target_pairs={{4,0},{8,4},{12,8},{16,12},{20,16},{24,20},{28,24},{32,28},{36,32}... | collective-permute-start | bytes 3145736 | tf_op jit(solution)/shard_map/while/body/eval_jaxpr/ppermute | solution.py:16
  1099.8 19.1 %collective-permute-start.1 = (f32[2,256,512]{2,1,0:T(8,128)S(1)}, f32[2,256,512]{2,1,0:T(8,128)S(1)}, u32[]{:S(2)}, u32[]{:S(2)}) collective-permute-start(f32[2,256,512]{2,1,0:T(8,128)S(1)} %get-tuple-element.308), channel_id=1, source_target_pairs={{4,0},{8,4},{12,8},{16,12},{20,16},{24,20},{28,24},{32,28},{36,32}... | collective-permute-start | bytes 3145736 | tf_op jit(solution)/shard_map/while/body/eval_jaxpr/ppermute | solution.py:16
  (58 other events, 409.7 us)
